TPU v7x, 256 devices: a whole 4x4x8 slice. The times are simulated.
256 devices in a mesh: tm: 16 (over z, x_lo), lon: 4 (over x_hi, core), lat: 4 (over y).
Axes of the slice: x: 4 (x_hi: 2, x_lo: 2; x = x_hi * 2 + x_lo), y: 4, z: 8, core: 2. Of those that a mesh axis runs over, the one named last changes fastest.
Arguments:
- iterate: float32 [16, 64, 64, 512], P('tm', None, 'lat', 'lon'), may hold values from -6 to 6
- heating: float32 [16, 64, 64, 512], P('tm', None, 'lat', 'lon'), may hold values from -6 to 6
- initial: float32 [64, 64, 512], P(None, 'lat', 'lon'), may hold values from -6 to 6
- region: int32 [64, 64, 512], P(None, 'lat', 'lon'), may hold values from 0 to 7
- cond_table: float32 [8], replicated, may hold values from 0.3 to 3
Outputs:
- updated: float32 [16, 64, 64, 512], P('tm', None, 'lat', 'lon')
Inputs may be any that keep to these rules, and one draw needn't show every extreme that they name: `region`: class index of each cell.
All inputs are finite; a program needn't handle non-finite values.
Results may differ from a plain program's by a relative error of at most 0.0003.
Values sent between devices are 32-bit elements; how exact they have to be, the bound alone decides.
A program may use at most 128 MiB of HBM per device.

v0:
```python
import jax
import jax.numpy as jnp
from jax import lax
from jax.sharding import PartitionSpec as P

SWEEPS = 4
corner_weight = 0.1


def padded(value, sides, width, wrap):
    for axis, dim in sides:
        peers, length = (lax.axis_size(axis), value.shape[dim])
        up = [(i, (i + 1) % peers) for i in range(peers if wrap else peers - 1)]
        down = [(j, i) for i, j in up]
        last = lax.slice_in_dim(value, length - width, length, axis=dim)
        initial = lax.slice_in_dim(value, 0, width, axis=dim)
        before = lax.ppermute(last, axis, up)
        after = lax.ppermute(initial, axis, down)
        value = jnp.concatenate([before, value, after], axis=dim)
    return value


def passed_along(block, axis, distance):
    devices = range(lax.axis_size(axis))
    route = [(i - distance, i) for i in devices if i - distance in devices]
    return lax.ppermute(block, axis, route)


def harmonic(first, second):
    return 2.0 * first * second / (first + second)


def conductivity(region, cond_table):
    classes = jnp.arange(cond_table.shape[0], dtype=jnp.int32)
    onehot = (region[..., None] == classes).astype(jnp.float32)
    return jnp.sum(onehot * cond_table, axis=-1)


def extend(stack):
    lat_ext = padded(stack, (("lat", 2),), 1, False)
    both = padded(lat_ext, (("lon", 3),), 1, True)
    return jnp.pad(both, ((0, 0), (1, 1), (0, 0), (0, 0)))


def face_weights(kext):
    centre = kext[1:-1, 1:-1, 1:-1]
    return (
        harmonic(centre, kext[:-2, 1:-1, 1:-1]),
        harmonic(centre, kext[2:, 1:-1, 1:-1]),
        harmonic(centre, kext[1:-1, :-2, 1:-1]),
        harmonic(centre, kext[1:-1, 2:, 1:-1]),
        harmonic(centre, kext[1:-1, 1:-1, :-2]),
        harmonic(centre, kext[1:-1, 1:-1, 2:]),
    )


def neighbours(weights, ext):
    near = weights[0] * ext[..., :-2, 1:-1, 1:-1] + weights[1] * ext[..., 2:, 1:-1, 1:-1]
    near = near + weights[2] * ext[..., 1:-1, :-2, 1:-1] + weights[3] * ext[..., 1:-1, 2:, 1:-1]
    near = near + weights[4] * ext[..., 1:-1, 1:-1, :-2] + weights[5] * ext[..., 1:-1, 1:-1, 2:]
    return near


def on_device(iterate, heating, initial, region, cond_table):
    steps = lax.axis_size("tm")
    own = lax.axis_index("tm")
    high = lax.Precision.HIGHEST
    kfield = conductivity(region, cond_table)
    ext = extend(jnp.stack([kfield, iterate[0]]))
    weights = face_weights(ext[0])
    total = weights[0] + weights[1] + weights[2] + weights[3] + weights[4] + weights[5]
    shifted = passed_along(iterate, "tm", 1)[0]
    previous = jnp.where(own == 0, initial, shifted)
    residual = heating[0] + previous - ((1.0 + total) * iterate[0] - neighbours(weights, ext[1]))
    scale_own = corner_weight ** (own.astype(jnp.float32) / steps)
    scaled = residual * scale_own
    zeros = jnp.zeros_like(residual)
    piece = lax.all_gather(scaled[None], "tm", axis=0, tiled=True)
    order = jnp.arange(piece.shape[0], dtype=jnp.int32)
    angle = 2.0 * jnp.pi / steps * (own * order % steps).astype(jnp.float32)
    real_part = jnp.einsum("n,nabc->abc", jnp.cos(angle), piece, precision=high)
    imag_part = (zeros, zeros)[1] - jnp.einsum("n,nabc->abc", jnp.sin(angle), piece, precision=high)
    beta = corner_weight ** (1.0 / steps)
    freq_angle = 2.0 * jnp.pi / steps * (own % steps).astype(jnp.float32)
    diag_re = 1.0 - beta * jnp.cos(freq_angle) + total
    diag_im = beta * jnp.sin(freq_angle) + zeros
    denom = diag_re * diag_re + diag_im * diag_im
    inv_re = diag_re / denom
    inv_im = -diag_im / denom
    sol_re = real_part * inv_re - imag_part * inv_im
    sol_im = real_part * inv_im + imag_part * inv_re
    for sweep in range(SWEEPS - 1):
        near = neighbours(weights, extend(jnp.stack([sol_re, sol_im])))
        rhs_re = real_part + near[0]
        rhs_im = imag_part + near[1]
        sol_re = rhs_re * inv_re - rhs_im * inv_im
        sol_im = rhs_re * inv_im + rhs_im * inv_re
    pieces = (
        lax.all_gather(sol_re[None], "tm", axis=0, tiled=True),
        lax.all_gather(sol_im[None], "tm", axis=0, tiled=True),
    )
    order = jnp.arange(pieces[0].shape[0], dtype=jnp.int32)
    angle = 2.0 * jnp.pi / steps * (order * own % steps).astype(jnp.float32)
    summed = jnp.einsum("k,kabc->abc", jnp.cos(angle), pieces[0], precision=high) - jnp.einsum(
        "k,kabc->abc", jnp.sin(angle), pieces[1], precision=high
    )
    back = summed / steps
    return iterate + (back / scale_own)[None]


def solution(mesh):
    return jax.shard_map(
        on_device,
        mesh=mesh,
        in_specs=(
            P("tm", None, "lat", "lon"),
            P("tm", None, "lat", "lon"),
            P(None, "lat", "lon"),
            P(None, "lat", "lon"),
            P(),
        ),
        out_specs=P("tm", None, "lat", "lon"),
        check_vma=False,
    )
```

profile of v0, /device:TPU:34, one launch (start us, length us, event | category | flops | bytes accessed | tf_op | source)
XLA Modules:
  0.0 730.6 jit_solution(5126643289084944055)
XLA Ops:
  10.2 3.5 collective-permute-start.1
  15.5 4.3 collective-permute-done.2
  25.1 3.3 collective-permute-start.4
  28.4 3.8 collective-permute-start
  34.6 4.0 select_maximum_fusion.15
  38.9 4.6 collective-permute-done
  43.5 3.9 fusion.45
  47.8 190.2 %all-gather.7.cloned.1.call-done = f32[1024,16,128]{2,1,0:T(8,128)} async-done(((f32[64,16,128]{2,1,0:T(8,128)}), f32[1024,16,128]{2,1,0:T(8,128)}) %all-gather.7.cloned.1.call-update) | async-done | bytes 8388624 | tf_op jit(solution)/shard_map/all_gather | solution.py:78
  238.0 12.6 %fusion.4 = f32[1,64,16,128]{3,0,2,1:T(1,128)S(1)} fusion(f32[16,64,16,128]{3,2,1,0:T(8,128)} %bitcast.108, s32[]{:T(128)S(6)} %axis_index.15), kind=kOutput, calls=%fused_computation.4 | convolution fusion | flops 25166048 | bytes 8912900 | tf_op jit(solution)/shard_map/n,nabc->abc/dot_general | solution.py:82
  250.6 7.8 %fusion.6 = f32[1,64,16,128]{3,0,2,1:T(1,128)S(1)} fusion(f32[16,64,16,128]{3,2,1,0:T(8,128)S(1)} %bitcast.109, s32[]{:T(128)S(6)} %axis_index.15), kind=kOutput, calls=%fused_computation.6 | convolution fusion | flops 25166048 | bytes 8912900 | tf_op jit(solution)/shard_map/n,nabc->abc/dot_general | solution.py:81
  259.1 3.4 collective-permute-start.5
  264.4 4.3 collective-permute-done.6
  273.1 3.3 collective-permute-start.8
  279.7 4.3 select_maximum_fusion.10
  286.9 3.4 collective-permute-start.9
  292.2 4.3 collective-permute-done.10
  307.3 4.3 select_maximum_fusion.5
  314.5 3.5 collective-permute-start.13
  319.9 4.3 collective-permute-done.14
  335.1 4.3 select_maximum_fusion
  343.9 181.1 %all-gather.11.cloned.1.call-done = f32[1024,16,128]{2,1,0:T(8,128)} async-done(((f32[64,16,128]{2,1,0:T(8,128)}), f32[1024,16,128]{2,1,0:T(8,128)}) %all-gather.11.cloned.1.call-update) | async-done | bytes 8388624 | tf_op jit(solution)/shard_map/all_gather | solution.py:100
  525.0 12.4 %fusion = f32[1,64,16,128]{3,0,2,1:T(1,128)S(1)} fusion(f32[16,64,16,128]{3,2,1,0:T(8,128)} %bitcast.120, s32[]{:T(128)S(6)} %axis_index.15), kind=kOutput, calls=%fused_computation | convolution fusion | flops 25166048 | bytes 8912900 | tf_op jit(solution)/shard_map/k,kabc->abc/dot_general | solution.py:104
  537.5 173.0 %all-gather.9.cloned.1.call-done = f32[1024,16,128]{2,1,0:T(8,128)} async-done(((f32[64,16,128]{2,1,0:T(8,128)}), f32[1024,16,128]{2,1,0:T(8,128)}) %all-gather.9.cloned.1.call-update) | async-done | bytes 8388624 | tf_op jit(solution)/shard_map/all_gather | solution.py:99
  710.5 12.5 %fusion.2 = f32[1,64,16,128]{3,0,2,1:T(1,128)S(1)} fusion(f32[16,64,16,128]{3,2,1,0:T(8,128)} %bitcast.121, s32[]{:T(128)S(6)} %axis_index.15), kind=kOutput, calls=%fused_computation.2 | convolution fusion | flops 25166048 | bytes 8912900 | tf_op jit(solution)/shard_map/k,kabc->abc/dot_general | solution.py:104
  (155 shorter events, 59.9 us)
Async XLA Ops:
  6.5 231.4 %all-gather.7.cloned.1.call-start = ((), (), s32[]{:S(2)}) async-start(), calls=%async_computation | async-start | bytes 8912896 | tf_op jit(solution)/shard_map/all_gather | solution.py:78
  10.2 5.4 collective-permute-start.1
  13.7 6.2 collective-permute-start.2
  24.6 7.7 %collective-permute-start.3 = (f32[2,64,18,1]{1,0,3,2:T(2,128)S(1)}, f32[2,64,18,1]{1,0,3,2:T(2,128)S(1)}, u32[]{:S(2)}, u32[]{:S(2)}) collective-permute-start(f32[2,64,18,1]{1,0,3,2:T(2,128)S(1)} %copy.57), channel_id=1, source_target_pairs={{0,4},{4,8},{8,12},{12,0},{1,5},{5,9},{9,13},{13,1},{2,6},{6,10},{... | collective-permute-start | bytes 27656 | tf_op jit(solution)/shard_map/ppermute | solution.py:17
  25.1 7.7 %collective-permute-start.4 = (f32[2,64,18,1]{1,0,3,2:T(2,128)S(1)}, f32[2,64,18,1]{1,0,3,2:T(2,128)S(1)}, u32[]{:S(2)}, u32[]{:S(2)}) collective-permute-start(f32[2,64,18,1]{1,0,3,2:T(2,128)S(1)} %copy.58), channel_id=1, source_target_pairs={{4,0},{8,4},{12,8},{0,12},{5,1},{9,5},{13,9},{1,13},{6,2},{10,6},{... | collective-permute-start | bytes 27656 | tf_op jit(solution)/shard_map/ppermute | solution.py:18
  28.4 15.0 %collective-permute-start = (f32[1,64,16,128]{3,2,1,0:T(8,128)S(1)}, f32[1,64,16,128]{3,2,1,0:T(8,128)}, u32[]{:S(2)}, u32[]{:S(2)}) collective-permute-start(f32[1,64,16,128]{3,2,1,0:T(8,128)S(1)} %copy-done.4), channel_id=1, source_target_pairs={{0,16},{16,32},{32,48},{48,64},{64,80},{80,96},{96,112},{112,128},... | collective-permute-start | bytes 1572872 | tf_op jit(solution)/shard_map/ppermute | solution.py:26
  47.4 211.1 %copy-start.18 = (f32[64,16,128]{2,1,0:T(8,128)}, f32[64,16,128]{2,1,0:T(8,128)S(1)}, u32[]{:S(2)}) copy-start(f32[64,16,128]{2,1,0:T(8,128)S(1)} %get-tuple-element.8) | copy-start | bytes 1572868
  47.4 211.1 %copy-start.22 = (f32[64,16,128]{2,1,0:T(8,128)}, f32[64,16,128]{2,1,0:T(8,128)S(1)}, u32[]{:S(2)}) copy-start(f32[64,16,128]{2,1,0:T(8,128)S(1)} %get-tuple-element.9) | copy-start | bytes 1572868
  47.4 211.1 %copy-start.26 = (f32[64,16,128]{2,1,0:T(8,128)}, f32[64,16,128]{2,1,0:T(8,128)S(1)}, u32[]{:S(2)}) copy-start(f32[64,16,128]{2,1,0:T(8,128)S(1)} %get-tuple-element.10) | copy-start | bytes 1572868
  47.4 477.6 %all-gather.11.cloned.1.call-start = ((), (), s32[]{:S(2)}) async-start(), calls=%async_computation.2 | async-start | bytes 8912896 | tf_op jit(solution)/shard_map/all_gather | solution.py:100
  238.0 12.6 %copy-start = (f32[1024,16,128]{2,1,0:T(8,128)S(1)}, f32[1024,16,128]{2,1,0:T(8,128)}, u32[]{:S(2)}) copy-start(f32[1024,16,128]{2,1,0:T(8,128)} %all-gather.7.cloned.1.call-done) | copy-start | bytes 25165828
  259.1 5.3 collective-permute-start.5
  262.5 6.2 collective-permute-start.6
  272.4 5.0 collective-permute-start.7
  273.1 4.8 collective-permute-start.8
  286.9 5.3 collective-permute-start.9
  290.3 6.2 collective-permute-start.10
  300.2 4.8 collective-permute-start.11
  301.4 4.1 collective-permute-start.12
  314.5 5.4 collective-permute-start.13
  318.0 6.2 collective-permute-start.14
  327.9 4.8 collective-permute-start.15
  329.6 3.7 collective-permute-start.16
  343.1 367.4 %all-gather.9.cloned.1.call-start = ((), (), s32[]{:S(2)}) async-start(), calls=%async_computation.1 | async-start | bytes 8912896 | tf_op jit(solution)/shard_map/all_gather | solution.py:99
  (40 other events, 230.7 us)
Sparse Core Ops, SparseCore 0:
  47.5 190.4 all-gather.6
  343.3 181.7 all-gather.10
  526.8 183.6 all-gather.8
where the time goes:
time: 738 us; the launch traced here: 731 us
  waiting for transfers between devices  572 us (78%)
  matrix products  45.4 us (6%)
  other arithmetic  37.1 us (5%)
  starting transfers between devices  36.8 us (5%)
  local copies, waits for them, and re-layouts  25.3 us (3%)
  between operations  14.4 us (2%)
    all_gather x1, waiting for transfers between devices, on_device(): piece = lax.all_gather(scaled[None], 'tm', axis=0, tiled=True)  190 us
    all_gather x1, waiting for transfers between devices, on_device(): lax.all_gather(sol_im[None], 'tm', axis=0, tiled=True)  181 us
    all_gather x1, waiting for transfers between devices, on_device(): lax.all_gather(sol_re[None], 'tm', axis=0, tiled=True)  173 us
    concatenate x8, other arithmetic, padded(): value = jnp.concatenate([before, value, after], axis=dim)  19 us
    ppermute x8, waiting for transfers between devices, padded(): after = lax.ppermute(initial, axis, down)  17.1 us
    ppermute x8, starting transfers between devices, padded(): after = lax.ppermute(initial, axis, down)  16.5 us
    ppermute x8, starting transfers between devices, padded(): before = lax.ppermute(last, axis, up)  16.1 us
  transfers between devices with their start and end apart: 20, of which 15 were waited for; matrix products, arithmetic and copies ran while one was open for 3% of the time, Pallas kernels for 0%

commit v1 on v0

--- a/solution.py
+++ b/solution.py
@@ -96,7 +96,9 @@
         sol_re = rhs_re * inv_re - rhs_im * inv_im
         sol_im = rhs_re * inv_im + rhs_im * inv_re
     pieces = (
-        lax.all_gather(sol_re[None], "tm", axis=0, tiled=True),
+        jnp.concatenate(
+            lax.all_to_all(jnp.stack([sol_re[None]] * lax.axis_size("tm")), "tm", 0, 0), axis=0
+        ),
         lax.all_gather(sol_im[None], "tm", axis=0, tiled=True),
     )
     order = jnp.arange(pieces[0].shape[0], dtype=jnp.int32)

time: 738 us -> 708 us (0.959)
  waiting for transfers between devices: 572 us -> 520 us
  local copies, waits for them, and re-layouts: 25.3 us -> 35.1 us
    all_gather x1 -> x0, waiting for transfers between devices: 173 us -> none  [on_device(): lax.all_gather(sol_re[None], 'tm', axis=0, tiled=True)]
    all_gather x1, waiting for transfers between devices: 181 us -> 304 us  [on_device(): lax.all_gather(sol_im[None], 'tm', axis=0, tiled=True)]
  transfers between devices with their start and end apart: 20 -> 20, of which waited for: 15 -> 14; matrix products, arithmetic and copies ran while one was open for 3% -> 4% of each run, Pallas kernels for 0% -> 0%
where the time goes in v1:
time: 708 us; the launch traced here: 695 us
  waiting for transfers between devices  520 us (73%)
  matrix products  45.4 us (6%)
  starting transfers between devices  43.3 us (6%)
  other arithmetic  36 us (5%)
  local copies, waits for them, and re-layouts  35.1 us (5%)
  between operations  14.7 us (2%)
    all_gather x1, waiting for transfers between devices, on_device(): lax.all_gather(sol_im[None], 'tm', axis=0, tiled=True)  304 us
    all_gather x1, waiting for transfers between devices, on_device(): piece = lax.all_gather(scaled[None], 'tm', axis=0, tiled=True)  190 us
    ppermute x8, waiting for transfers between devices, padded(): after = lax.ppermute(initial, axis, down)  19.7 us
    concatenate x8, other arithmetic, padded(): value = jnp.concatenate([before, value, after], axis=dim)  19 us
    ppermute x8, starting transfers between devices, padded(): after = lax.ppermute(initial, axis, down)  16.9 us
    ppermute x8, starting transfers between devices, padded(): before = lax.ppermute(last, axis, up)  15.7 us
    slice x8, local copies, waits for them, and re-layouts, padded(): last = lax.slice_in_dim(value, length - width, length, axis=dim)  15.4 us
  transfers between devices with their start and end apart: 20, of which 14 were waited for; matrix products, arithmetic and copies ran while one was open for 4% of the time, Pallas kernels for 0%

profile of v1, /device:TPU:34, one launch (start us, length us, event | category | flops | bytes accessed | tf_op | source)
XLA Modules:
  0.0 694.6 jit_solution(13261720924664742175)
XLA Ops:
  10.2 3.5 collective-permute-start.1
  15.5 4.3 collective-permute-done.2
  25.1 3.3 collective-permute-start.4
  28.4 3.8 collective-permute-start
  34.6 4.0 select_maximum_fusion.15
  38.9 4.6 collective-permute-done
  46.9 190.2 %all-gather.5.cloned.1.call-done = f32[1024,16,128]{2,1,0:T(8,128)} async-done(((f32[64,16,128]{2,1,0:T(8,128)}), f32[1024,16,128]{2,1,0:T(8,128)}) %all-gather.5.cloned.1.call-update) | async-done | bytes 8388624 | tf_op jit(solution)/shard_map/all_gather | solution.py:78
  237.2 12.6 %fusion.4 = f32[1,64,16,128]{3,0,2,1:T(1,128)S(1)} fusion(f32[16,64,16,128]{3,2,1,0:T(8,128)} %bitcast.108, s32[]{:T(128)S(6)} %axis_index.15), kind=kOutput, calls=%fused_computation.4 | convolution fusion | flops 25166048 | bytes 8912900 | tf_op jit(solution)/shard_map/n,nabc->abc/dot_general | solution.py:82
  249.8 7.8 %fusion.6 = f32[1,64,16,128]{3,0,2,1:T(1,128)S(1)} fusion(f32[16,64,16,128]{3,2,1,0:T(8,128)S(1)} %bitcast.109, s32[]{:T(128)S(6)} %axis_index.15), kind=kOutput, calls=%fused_computation.6 | convolution fusion | flops 25166048 | bytes 8912900 | tf_op jit(solution)/shard_map/n,nabc->abc/dot_general | solution.py:81
  258.3 3.4 collective-permute-start.5
  263.6 4.3 collective-permute-done.6
  274.2 3.3 collective-permute-start.8
  280.7 4.3 select_maximum_fusion.10
  287.9 3.4 collective-permute-start.9
  293.2 4.3 collective-permute-done.10
  310.1 4.3 select_maximum_fusion.5
  317.3 3.1 collective-permute-start.13
  322.3 4.3 collective-permute-done.14
  339.2 4.3 select_maximum_fusion
  347.1 4.1 stack.47
  351.3 6.7 all-to-all-start
  357.9 303.8 %all-gather.7.cloned.1.call-done = f32[1024,16,128]{2,1,0:T(8,128)} async-done(((f32[64,16,128]{2,1,0:T(8,128)}), f32[1024,16,128]{2,1,0:T(8,128)}) %all-gather.7.cloned.1.call-update) | async-done | bytes 8388624 | tf_op jit(solution)/shard_map/all_gather | solution.py:102
  661.7 12.4 %fusion = f32[1,64,16,128]{3,0,2,1:T(1,128)S(1)} fusion(f32[16,64,16,128]{3,2,1,0:T(8,128)} %bitcast.120, s32[]{:T(128)S(6)} %axis_index.15), kind=kOutput, calls=%fused_computation | convolution fusion | flops 25166048 | bytes 8912900 | tf_op jit(solution)/shard_map/k,kabc->abc/dot_general | solution.py:106
  674.2 12.5 %fusion.2 = f32[1,64,16,128]{3,0,2,1:T(1,128)S(1)} fusion(f32[16,64,16,128]{3,2,1,0:T(8,128)} %bitcast.29, s32[]{:T(128)S(6)} %axis_index.15), kind=kOutput, calls=%fused_computation.2 | convolution fusion | flops 25166048 | bytes 8912900 | tf_op jit(solution)/shard_map/k,kabc->abc/dot_general | solution.py:106
  (155 shorter events, 67.4 us)
Async XLA Ops:
  6.5 230.6 %all-gather.5.cloned.1.call-start = ((), (), s32[]{:S(2)}) async-start(), calls=%async_computation.1 | async-start | bytes 8912896 | tf_op jit(solution)/shard_map/all_gather | solution.py:78
  10.2 5.4 collective-permute-start.1
  13.7 6.2 collective-permute-start.2
  24.6 7.7 %collective-permute-start.3 = (f32[2,64,18,1]{1,0,3,2:T(2,128)S(1)}, f32[2,64,18,1]{1,0,3,2:T(2,128)S(1)}, u32[]{:S(2)}, u32[]{:S(2)}) collective-permute-start(f32[2,64,18,1]{1,0,3,2:T(2,128)S(1)} %copy.57), channel_id=1, source_target_pairs={{0,4},{4,8},{8,12},{12,0},{1,5},{5,9},{9,13},{13,1},{2,6},{6,10},{... | collective-permute-start | bytes 27656 | tf_op jit(solution)/shard_map/ppermute | solution.py:17
  25.1 7.7 %collective-permute-start.4 = (f32[2,64,18,1]{1,0,3,2:T(2,128)S(1)}, f32[2,64,18,1]{1,0,3,2:T(2,128)S(1)}, u32[]{:S(2)}, u32[]{:S(2)}) collective-permute-start(f32[2,64,18,1]{1,0,3,2:T(2,128)S(1)} %copy.58), channel_id=1, source_target_pairs={{4,0},{8,4},{12,8},{0,12},{5,1},{9,5},{13,9},{1,13},{6,2},{10,6},{... | collective-permute-start | bytes 27656 | tf_op jit(solution)/shard_map/ppermute | solution.py:18
  28.4 15.0 %collective-permute-start = (f32[1,64,16,128]{3,2,1,0:T(8,128)S(1)}, f32[1,64,16,128]{3,2,1,0:T(8,128)S(1)}, u32[]{:S(2)}, u32[]{:S(2)}) collective-permute-start(f32[1,64,16,128]{3,2,1,0:T(8,128)S(1)} %copy-done.4), channel_id=1, source_target_pairs={{0,16},{16,32},{32,48},{48,64},{64,80},{80,96},{96,112},{112,128},... | collective-permute-start | bytes 1572872 | tf_op jit(solution)/shard_map/ppermute | solution.py:26
  46.5 211.1 %copy-start.18 = (f32[64,16,128]{2,1,0:T(8,128)}, f32[64,16,128]{2,1,0:T(8,128)S(1)}, u32[]{:S(2)}) copy-start(f32[64,16,128]{2,1,0:T(8,128)S(1)} %get-tuple-element.8) | copy-start | bytes 1572868
  46.5 211.1 %copy-start.22 = (f32[64,16,128]{2,1,0:T(8,128)}, f32[64,16,128]{2,1,0:T(8,128)S(1)}, u32[]{:S(2)}) copy-start(f32[64,16,128]{2,1,0:T(8,128)S(1)} %get-tuple-element.9) | copy-start | bytes 1572868
  46.6 615.2 %all-gather.7.cloned.1.call-start = ((), (), s32[]{:S(2)}) async-start(), calls=%async_computation.2 | async-start | bytes 8912896 | tf_op jit(solution)/shard_map/all_gather | solution.py:102
  237.2 12.6 %copy-start = (f32[1024,16,128]{2,1,0:T(8,128)S(1)}, f32[1024,16,128]{2,1,0:T(8,128)}, u32[]{:S(2)}) copy-start(f32[1024,16,128]{2,1,0:T(8,128)} %all-gather.5.cloned.1.call-done) | copy-start | bytes 25165828
  258.3 5.3 collective-permute-start.5
  261.7 6.2 collective-permute-start.6
  272.1 5.4 collective-permute-start.7
  274.2 4.8 collective-permute-start.8
  287.9 5.3 collective-permute-start.9
  291.3 6.2 collective-permute-start.10
  301.7 5.2 collective-permute-start.11
  304.3 4.0 collective-permute-start.12
  317.3 5.0 collective-permute-start.13
  320.4 6.2 collective-permute-start.14
  330.8 5.2 collective-permute-start.15
  333.9 3.6 collective-permute-start.16
  351.3 322.9 %all-to-all-start = ((f32[16,1,64,16,128]{4,3,2,1,0:T(8,128)}), f32[16,1,64,16,128]{4,3,2,1,0:T(8,128)}, u32[]{:S(2)}, u32[]{:S(2)}) async-start(f32[16,1,64,16,128]{4,3,2,1,0:T(8,128)} %stack.47), calls=%async_computation | async-start | bytes 16777216 | tf_op jit(solution)/shard_map/all_to_all | solution.py:100
  674.2 12.5 %copy-start.5 = (f32[1,64,16,128]{3,2,1,0:T(8,128)S(1)}, f32[1,64,16,128]{3,2,1,0:T(8,128)}, u32[]{:S(2)}) copy-start(f32[1,64,16,128]{3,2,1,0:T(8,128)} %param.5) | copy-start | bytes 1572868
  (40 other events, 239.6 us)
Sparse Core Ops, SparseCore 0:
  46.7 190.4 all-gather.4
  347.2 314.4 all-gather.6
